TPU v7x, 256 devices: a whole 4x4x8 slice. The times are simulated.
256 devices in a mesh: seq: 32 (over z, x), blk: 8 (over y, core).
Axes of the slice: x: 4, y: 4, z: 8, core: 2. Of those that a mesh axis runs over, the one named last changes fastest.
Arguments:
- qkv: bfloat16 [32768, 12288], P(('seq', 'blk')), may hold values from -24 to 24
- kept_kv: bfloat16 [32, 2, 128, 4096], P('blk', None, None, 'seq'), may hold values from -24 to 24
- cur_list: int32 [256, 8], replicated, may hold values from 0 to 255, as said below
- kept_list: int32 [256, 12], replicated, may hold values from 0 to 31, as said below
- kept_count: int32 [256], replicated, may hold values from 1 to 12, as said below
Outputs:
- attn_out: bfloat16 [32768, 4096], P(('seq', 'blk'))
Inputs may be any that keep to these rules, and one draw needn't show every extreme that they name: `cur_list`: row t lists 8 different tiles t2 of tile t's spatial region, that is with (t2) % 8 equal to (t) % 8; the first entry is t itself. `kept_list`: each row names 12 different kept blocks. `kept_count`: some tile uses all 12 slots.
All inputs are finite; a program needn't handle non-finite values.
Results may differ from a plain program's by a relative error of at most 0.0025.
Values may be sent and summed in bfloat16 or wider, within the bound.
A program may use at most 64 MiB of HBM per device.

v0:
```python
import math
import jax
import jax.numpy as jnp
from jax import lax
from jax.sharding import PartitionSpec as P

HEAD_DIM = 128
MASKED_SCORE = -1e30


def per_device(qkv, kept_kv, cur_list, kept_list, kept_count):
    seq_count = lax.axis_size("seq")
    blk_count = lax.axis_size("blk")
    tok_rows = qkv.shape[0]
    head_width = HEAD_DIM
    head_total = qkv.shape[1] // (3 * head_width)
    tile_len = kept_kv.shape[2]
    tiles_dev = tok_rows // tile_len
    shaped = qkv.reshape(tok_rows, 3, head_total, head_width)
    arrived = lax.all_to_all(shaped, "seq", split_axis=2, concat_axis=0, tiled=True)
    head_dev = arrived.shape[2]
    tile_mine = seq_count * tiles_dev
    grouped = arrived.reshape(tile_mine, tile_len, 3, head_dev, head_width)
    ordered = jnp.transpose(grouped, (2, 0, 3, 1, 4))
    queries_all = ordered[0]
    near_keys_all = ordered[1]
    near_values_all = ordered[2]
    kept_all = lax.all_gather(kept_kv, "blk", axis=0, tiled=True)
    kept_all = jnp.transpose(
        kept_all.reshape(kept_all.shape[0], 2, tile_len, head_dev, head_width), (0, 1, 3, 2, 4)
    )
    far_keys_all = kept_all[:, 0]
    far_values_all = kept_all[:, 1]
    region = lax.axis_index("blk")
    local_ids = jnp.arange(tile_mine, dtype=jnp.int32)
    tile_ids = (local_ids // tiles_dev * blk_count + region) * tiles_dev + local_ids % tiles_dev
    cur_ids = cur_list[tile_ids]
    cur_local = cur_ids // tiles_dev // blk_count * tiles_dev + cur_ids % tiles_dev
    kept_ids = kept_list[tile_ids]
    slot_counts = kept_count[tile_ids]
    score_scale = 1.0 / math.sqrt(head_width)
    window_slots = kept_ids.shape[1]
    near_count = cur_local.shape[1]
    tiles_step = 4
    step_total = tile_mine // tiles_step

    def attend(pieces):
        queries, cur_sel, kept_sel, slot_count = pieces
        near_keys = near_keys_all[cur_sel]
        near_values = near_values_all[cur_sel]
        near_scores = (
            jnp.einsum("bhid,bnhkd->bhink", queries, near_keys, preferred_element_type=jnp.float32)
            * score_scale
        )
        near_max = near_scores.max(axis=(3, 4))[..., None, None]
        far_keys = far_keys_all[kept_sel]
        far_values = far_values_all[kept_sel]
        far_scores = (
            jnp.einsum("bhid,bwhkd->bhiwk", queries, far_keys, preferred_element_type=jnp.float32)
            * score_scale
        )
        is_live = (jnp.arange(window_slots)[None, :] < slot_count[:, None])[:, None, None, :, None]
        far_scores = jnp.where(is_live, far_scores, MASKED_SCORE)
        row_max = jnp.maximum(near_max, far_scores.max(axis=(3, 4))[..., None, None])
        near_weights = jnp.exp(near_scores - row_max)
        far_weights = jnp.where(is_live, jnp.exp(far_scores - row_max), 0.0)
        row_total = near_weights.sum(axis=(3, 4)) + far_weights.sum(axis=(3, 4))
        mixture = jnp.einsum(
            "bhink,bnhkd->bhid",
            near_weights.astype(jnp.bfloat16),
            near_values,
            preferred_element_type=jnp.float32,
        )
        mixture = mixture + jnp.einsum(
            "bhiwk,bwhkd->bhid",
            far_weights.astype(jnp.bfloat16),
            far_values,
            preferred_element_type=jnp.float32,
        )
        result_rows = (mixture / row_total[..., None]).astype(jnp.bfloat16)
        return jnp.transpose(result_rows, (0, 2, 1, 3))

    attended = lax.map(
        attend,
        (
            queries_all.reshape(step_total, tiles_step, head_dev, tile_len, head_width),
            cur_local.reshape(step_total, tiles_step, near_count),
            kept_ids.reshape(step_total, tiles_step, window_slots),
            slot_counts.reshape(step_total, tiles_step),
        ),
    )
    attended = attended.reshape(seq_count * tok_rows, head_dev, head_width)
    returned = lax.all_to_all(attended, "seq", split_axis=0, concat_axis=1, tiled=True)
    return returned.reshape(tok_rows, head_total * head_width)


def solution(mesh):
    placed = (P(("seq", "blk"), None), P("blk", None, None, "seq"), P(), P(), P())
    return jax.shard_map(
        per_device, mesh=mesh, in_specs=placed, out_specs=P(("seq", "blk"), None), check_vma=False
    )
```

profile of v0, /device:TPU:2, one launch (start us, length us, event | category | flops | bytes accessed | tf_op | source)
XLA Modules:
  0.0 308.9 jit_solution(16223919463636740690)
XLA Ops:
  6.5 3.5 %copy.45 = bf16[128,12288]{0,1:T(8,128)(2,1)S(1)} copy(bf16[128,12288]{1,0:T(8,128)(2,1)} %param.7) | data formatting | bytes 6291456 | tf_op args[0]
  11.9 11.7 %all-to-all-start = ((bf16[128,3,32,128]{0,3,1,2:T(8,128)(2,1)}), bf16[128,3,32,128]{0,3,1,2:T(8,128)(2,1)S(1)}, u32[]{:S(2)}, u32[]{:S(2)}) async-start(bf16[128,3,32,128]{0,3,1,2:T(8,128)(2,1)} %copy.46), calls=%async_computation | async-start | bytes 6291456 | tf_op jit(solution)/shard_map/all_to_all | solution.py:20
  26.8 28.6 %all-gather.2.cloned.1.call-done = bf16[32,2,128,128]{3,2,0,1:T(8,128)(2,1)} async-done(((bf16[4,2,128,128]{3,2,0,1:T(8,128)(2,1)}), bf16[32,2,128,128]{3,2,0,1:T(8,128)(2,1)}) %all-gather.2.cloned.1.call-update) | async-done | bytes 2097168 | tf_op jit(solution)/shard_map/all_gather | solution.py:28
  58.5 36.5 %all-to-all-done = bf16[128,3,32,128]{0,3,1,2:T(8,128)(2,1)S(1)} async-done(((bf16[128,3,32,128]{0,3,1,2:T(8,128)(2,1)}), bf16[128,3,32,128]{0,3,1,2:T(8,128)(2,1)S(1)}, u32[]{:S(2)}, u32[]{:S(2)}) %all-to-all-start) | async-done | bytes 3145760 | tf_op jit(solution)/shard_map/all_to_all | solution.py:20
  100.3 160.1 %while.10 = (s32[]{:T(128)}, bf16[8,4,128,1,128]{4,2,1,3,0:T(8,128)(2,1)}, bf16[8,4,1,128,128]{3,4,1,0,2:T(8,128)(2,1)}, s32[8,4,8]{2,1,0:T(4,128)S(1)}, bf16[32...) while((s32[]{:T(128)}, ...), condition=%wide.region_5.6_spmd, body=%wide.region_0.5_spmd.sunk | while | flops 685704448 | bytes 57583712 | solution.py:83
  102.6 3.1 %fusion.67 = (f32[4,128]{1,0:T(4,128)S(1)}, f32[4,128,12,128]{1,3,2,0:T(8,128)}) fusion(pred[4,12]{1,0:T(4,128)(4,1)S(1)} %iota_compare_fusion.2, bf16[4,12,128,128]{3,2,1,0:T(8,128)(2,1)S(1)} %bitcast.120, bf16[8,4,1,128,128]{3,4,1,0,2:T(8,128)(2,1)} %get-tuple-element.220, s32[]{:T(128)} %get-tuple-element.207), kind=kOutput, calls=%fused_computation.9.clone.1 | convolution fusion | flops 203685376 | bytes 4852272 | tf_op jit(solution)/shard_map/while/body/eval_jaxpr/bhid,bwhkd->bhiwk/dot_general | solution.py:59
  113.7 3.4 %gather_fusion.3 = bf16[48,128,128]{2,1,0:T(8,128)(2,1)} fusion(bf16[32,128,128]{2,1,0:T(8,128)(2,1)} %bitcast.123, s32[1024]{0:T(1024)S(1)} %pad_clamp_fusion.6), kind=kCustom, calls=%fused_computation.3.clone.1 | custom fusion | bytes 3145920 | tf_op jit(solution)/shard_map/while/body/eval_jaxpr/gather | solution.py:57
  117.1 3.2 %fusion.70 = bf16[8,4,128,1,128]{4,2,1,3,0:T(8,128)(2,1)} fusion(bf16[8,4,128,1,128]{4,2,1,3,0:T(8,128)(2,1)} %get-tuple-element.208, s32[]{:T(128)} %get-tuple-element.207, f32[4,128,128]{2,1,0:T(8,128)S(1)} %convolution_bitcast_fusion.2, bf16[4,12,128,128]{3,2,1,0:T(8,128)(2,1)} %bitcast.124, f32[4,128,12,128]{1,3,2,0:T(8,128)S(1)} %copy-done.2, ...), kind=kOutput, calls=%fused_computation.24.clone.1 | convolution fusion | flops 205455360 | bytes 5116464 | tf_op jit(solution)/shard_map/while/body/eval_jaxpr/bhiwk,bwhkd->bhid/dot_general | solution.py:74
  122.6 3.1 %fusion.67 = (f32[4,128]{1,0:T(4,128)S(1)}, f32[4,128,12,128]{1,3,2,0:T(8,128)}) fusion(pred[4,12]{1,0:T(4,128)(4,1)S(1)} %iota_compare_fusion.2, bf16[4,12,128,128]{3,2,1,0:T(8,128)(2,1)S(1)} %bitcast.120, bf16[8,4,1,128,128]{3,4,1,0,2:T(8,128)(2,1)} %get-tuple-element.220, s32[]{:T(128)} %get-tuple-element.207), kind=kOutput, calls=%fused_computation.9.clone.1 | convolution fusion | flops 203685376 | bytes 4852272 | tf_op jit(solution)/shard_map/while/body/eval_jaxpr/bhid,bwhkd->bhiwk/dot_general | solution.py:59
  133.7 3.4 %gather_fusion.3 = bf16[48,128,128]{2,1,0:T(8,128)(2,1)} fusion(bf16[32,128,128]{2,1,0:T(8,128)(2,1)} %bitcast.123, s32[1024]{0:T(1024)S(1)} %pad_clamp_fusion.6), kind=kCustom, calls=%fused_computation.3.clone.1 | custom fusion | bytes 3145920 | tf_op jit(solution)/shard_map/while/body/eval_jaxpr/gather | solution.py:57
  137.1 3.2 %fusion.70 = bf16[8,4,128,1,128]{4,2,1,3,0:T(8,128)(2,1)} fusion(bf16[8,4,128,1,128]{4,2,1,3,0:T(8,128)(2,1)} %get-tuple-element.208, s32[]{:T(128)} %get-tuple-element.207, f32[4,128,128]{2,1,0:T(8,128)S(1)} %convolution_bitcast_fusion.2, bf16[4,12,128,128]{3,2,1,0:T(8,128)(2,1)} %bitcast.124, f32[4,128,12,128]{1,3,2,0:T(8,128)S(1)} %copy-done.2, ...), kind=kOutput, calls=%fused_computation.24.clone.1 | convolution fusion | flops 205455360 | bytes 5116464 | tf_op jit(solution)/shard_map/while/body/eval_jaxpr/bhiwk,bwhkd->bhid/dot_general | solution.py:74
  153.7 3.4 %gather_fusion.3 = bf16[48,128,128]{2,1,0:T(8,128)(2,1)} fusion(bf16[32,128,128]{2,1,0:T(8,128)(2,1)} %bitcast.123, s32[1024]{0:T(1024)S(1)} %pad_clamp_fusion.6), kind=kCustom, calls=%fused_computation.3.clone.1 | custom fusion | bytes 3145920 | tf_op jit(solution)/shard_map/while/body/eval_jaxpr/gather | solution.py:57
  157.1 3.2 %fusion.70 = bf16[8,4,128,1,128]{4,2,1,3,0:T(8,128)(2,1)} fusion(bf16[8,4,128,1,128]{4,2,1,3,0:T(8,128)(2,1)} %get-tuple-element.208, s32[]{:T(128)} %get-tuple-element.207, f32[4,128,128]{2,1,0:T(8,128)S(1)} %convolution_bitcast_fusion.2, bf16[4,12,128,128]{3,2,1,0:T(8,128)(2,1)} %bitcast.124, f32[4,128,12,128]{1,3,2,0:T(8,128)S(1)} %copy-done.2, ...), kind=kOutput, calls=%fused_computation.24.clone.1 | convolution fusion | flops 205455360 | bytes 5116464 | tf_op jit(solution)/shard_map/while/body/eval_jaxpr/bhiwk,bwhkd->bhid/dot_general | solution.py:74
  173.7 3.4 %gather_fusion.3 = bf16[48,128,128]{2,1,0:T(8,128)(2,1)} fusion(bf16[32,128,128]{2,1,0:T(8,128)(2,1)} %bitcast.123, s32[1024]{0:T(1024)S(1)} %pad_clamp_fusion.6), kind=kCustom, calls=%fused_computation.3.clone.1 | custom fusion | bytes 3145920 | tf_op jit(solution)/shard_map/while/body/eval_jaxpr/gather | solution.py:57
  177.2 3.2 %fusion.70 = bf16[8,4,128,1,128]{4,2,1,3,0:T(8,128)(2,1)} fusion(bf16[8,4,128,1,128]{4,2,1,3,0:T(8,128)(2,1)} %get-tuple-element.208, s32[]{:T(128)} %get-tuple-element.207, f32[4,128,128]{2,1,0:T(8,128)S(1)} %convolution_bitcast_fusion.2, bf16[4,12,128,128]{3,2,1,0:T(8,128)(2,1)} %bitcast.124, f32[4,128,12,128]{1,3,2,0:T(8,128)S(1)} %copy-done.2, ...), kind=kOutput, calls=%fused_computation.24.clone.1 | convolution fusion | flops 205455360 | bytes 5116464 | tf_op jit(solution)/shard_map/while/body/eval_jaxpr/bhiwk,bwhkd->bhid/dot_general | solution.py:74
  193.8 3.4 %gather_fusion.3 = bf16[48,128,128]{2,1,0:T(8,128)(2,1)} fusion(bf16[32,128,128]{2,1,0:T(8,128)(2,1)} %bitcast.123, s32[1024]{0:T(1024)S(1)} %pad_clamp_fusion.6), kind=kCustom, calls=%fused_computation.3.clone.1 | custom fusion | bytes 3145920 | tf_op jit(solution)/shard_map/while/body/eval_jaxpr/gather | solution.py:57
  197.2 3.2 %fusion.70 = bf16[8,4,128,1,128]{4,2,1,3,0:T(8,128)(2,1)} fusion(bf16[8,4,128,1,128]{4,2,1,3,0:T(8,128)(2,1)} %get-tuple-element.208, s32[]{:T(128)} %get-tuple-element.207, f32[4,128,128]{2,1,0:T(8,128)S(1)} %convolution_bitcast_fusion.2, bf16[4,12,128,128]{3,2,1,0:T(8,128)(2,1)} %bitcast.124, f32[4,128,12,128]{1,3,2,0:T(8,128)S(1)} %copy-done.2, ...), kind=kOutput, calls=%fused_computation.24.clone.1 | convolution fusion | flops 205455360 | bytes 5116464 | tf_op jit(solution)/shard_map/while/body/eval_jaxpr/bhiwk,bwhkd->bhid/dot_general | solution.py:74
  213.8 3.4 %gather_fusion.3 = bf16[48,128,128]{2,1,0:T(8,128)(2,1)} fusion(bf16[32,128,128]{2,1,0:T(8,128)(2,1)} %bitcast.123, s32[1024]{0:T(1024)S(1)} %pad_clamp_fusion.6), kind=kCustom, calls=%fused_computation.3.clone.1 | custom fusion | bytes 3145920 | tf_op jit(solution)/shard_map/while/body/eval_jaxpr/gather | solution.py:57
  217.2 3.2 %fusion.70 = bf16[8,4,128,1,128]{4,2,1,3,0:T(8,128)(2,1)} fusion(bf16[8,4,128,1,128]{4,2,1,3,0:T(8,128)(2,1)} %get-tuple-element.208, s32[]{:T(128)} %get-tuple-element.207, f32[4,128,128]{2,1,0:T(8,128)S(1)} %convolution_bitcast_fusion.2, bf16[4,12,128,128]{3,2,1,0:T(8,128)(2,1)} %bitcast.124, f32[4,128,12,128]{1,3,2,0:T(8,128)S(1)} %copy-done.2, ...), kind=kOutput, calls=%fused_computation.24.clone.1 | convolution fusion | flops 205455360 | bytes 5116464 | tf_op jit(solution)/shard_map/while/body/eval_jaxpr/bhiwk,bwhkd->bhid/dot_general | solution.py:74
  233.8 3.4 %gather_fusion.3 = bf16[48,128,128]{2,1,0:T(8,128)(2,1)} fusion(bf16[32,128,128]{2,1,0:T(8,128)(2,1)} %bitcast.123, s32[1024]{0:T(1024)S(1)} %pad_clamp_fusion.6), kind=kCustom, calls=%fused_computation.3.clone.1 | custom fusion | bytes 3145920 | tf_op jit(solution)/shard_map/while/body/eval_jaxpr/gather | solution.py:57
  237.2 3.2 %fusion.70 = bf16[8,4,128,1,128]{4,2,1,3,0:T(8,128)(2,1)} fusion(bf16[8,4,128,1,128]{4,2,1,3,0:T(8,128)(2,1)} %get-tuple-element.208, s32[]{:T(128)} %get-tuple-element.207, f32[4,128,128]{2,1,0:T(8,128)S(1)} %convolution_bitcast_fusion.2, bf16[4,12,128,128]{3,2,1,0:T(8,128)(2,1)} %bitcast.124, f32[4,128,12,128]{1,3,2,0:T(8,128)S(1)} %copy-done.2, ...), kind=kOutput, calls=%fused_computation.24.clone.1 | convolution fusion | flops 205455360 | bytes 5116464 | tf_op jit(solution)/shard_map/while/body/eval_jaxpr/bhiwk,bwhkd->bhid/dot_general | solution.py:74
  253.8 3.4 %gather_fusion.3 = bf16[48,128,128]{2,1,0:T(8,128)(2,1)} fusion(bf16[32,128,128]{2,1,0:T(8,128)(2,1)} %bitcast.123, s32[1024]{0:T(1024)S(1)} %pad_clamp_fusion.6), kind=kCustom, calls=%fused_computation.3.clone.1 | custom fusion | bytes 3145920 | tf_op jit(solution)/shard_map/while/body/eval_jaxpr/gather | solution.py:57
  257.2 3.2 %fusion.70 = bf16[8,4,128,1,128]{4,2,1,3,0:T(8,128)(2,1)} fusion(bf16[8,4,128,1,128]{4,2,1,3,0:T(8,128)(2,1)} %get-tuple-element.208, s32[]{:T(128)} %get-tuple-element.207, f32[4,128,128]{2,1,0:T(8,128)S(1)} %convolution_bitcast_fusion.2, bf16[4,12,128,128]{3,2,1,0:T(8,128)(2,1)} %bitcast.124, f32[4,128,12,128]{1,3,2,0:T(8,128)S(1)} %copy-done.2, ...), kind=kOutput, calls=%fused_computation.24.clone.1 | convolution fusion | flops 205455360 | bytes 5116464 | tf_op jit(solution)/shard_map/while/body/eval_jaxpr/bhiwk,bwhkd->bhid/dot_general | solution.py:74
  264.0 34.9 %all_to_all.27 = bf16[32,2,8192]{2,1,0:T(2,128)(2,1)S(1)} all-to-all(bf16[32,2,8192]{2,1,0:T(2,128)(2,1)S(1)} %reshape.276), channel_id=1, replica_groups=mesh['seq'=32,'blk'=8] {'seq'}, dimensions={0} | all-to-all | bytes 2097152 | tf_op jit(solution)/shard_map/all_to_all | solution.py:93
  (209 shorter events, 120.1 us)
Async XLA Ops:
  6.5 19.4 %copy-start = (s32[256]{0:T(256)S(1)}, s32[256]{0:T(256)}, u32[]{:S(2)}) copy-start(s32[256]{0:T(256)} %param.11) | copy-start | bytes 3076
  11.9 11.8 %copy-start.4 = (bf16[4,2,128,128]{3,2,1,0:T(8,128)(2,1)S(1)}, bf16[4,2,128,128]{3,2,1,0:T(8,128)(2,1)}, u32[]{:S(2)}) copy-start(bf16[4,2,128,128]{3,2,1,0:T(8,128)(2,1)} %param.8) | copy-start | bytes 786436
  11.9 12.6 %copy-start.6 = (s32[256,8]{0,1:T(8,128)S(1)}, s32[256,8]{0,1:T(8,128)}, u32[]{:S(2)}) copy-start(s32[256,8]{0,1:T(8,128)} %param.9) | copy-start | bytes 24580
  11.9 12.7 %copy-start.5 = (s32[256,12]{0,1:T(8,128)S(1)}, s32[256,12]{0,1:T(8,128)}, u32[]{:S(2)}) copy-start(s32[256,12]{0,1:T(8,128)} %param.10) | copy-start | bytes 36868
  11.9 83.0 %all-to-all-start = ((bf16[128,3,32,128]{0,3,1,2:T(8,128)(2,1)}), bf16[128,3,32,128]{0,3,1,2:T(8,128)(2,1)S(1)}, u32[]{:S(2)}, u32[]{:S(2)}) async-start(bf16[128,3,32,128]{0,3,1,2:T(8,128)(2,1)} %copy.46), calls=%async_computation | async-start | bytes 6291456 | tf_op jit(solution)/shard_map/all_to_all | solution.py:20
  23.7 31.7 %all-gather.2.cloned.1.call-start = ((), (), s32[]{:S(2)}) async-start(), calls=%async_computation.2 | async-start | bytes 2359296 | tf_op jit(solution)/shard_map/all_gather | solution.py:28
  96.7 2.3 copy-start.3
  107.8 2.0 copy-start.1
  113.7 3.4 %copy-start.2 = (f32[4,128,12,128]{1,3,2,0:T(8,128)S(1)}, f32[4,128,12,128]{1,3,2,0:T(8,128)}, u32[]{:S(2)}) copy-start(f32[4,128,12,128]{1,3,2,0:T(8,128)} %get-tuple-element.195) | copy-start | bytes 9437188 | tf_op jit(solution)/shard_map/while
  127.8 2.0 copy-start.1
  133.7 3.4 %copy-start.2 = (f32[4,128,12,128]{1,3,2,0:T(8,128)S(1)}, f32[4,128,12,128]{1,3,2,0:T(8,128)}, u32[]{:S(2)}) copy-start(f32[4,128,12,128]{1,3,2,0:T(8,128)} %get-tuple-element.195) | copy-start | bytes 9437188 | tf_op jit(solution)/shard_map/while
  147.8 2.0 copy-start.1
  153.7 3.4 %copy-start.2 = (f32[4,128,12,128]{1,3,2,0:T(8,128)S(1)}, f32[4,128,12,128]{1,3,2,0:T(8,128)}, u32[]{:S(2)}) copy-start(f32[4,128,12,128]{1,3,2,0:T(8,128)} %get-tuple-element.195) | copy-start | bytes 9437188 | tf_op jit(solution)/shard_map/while
  167.9 2.0 copy-start.1
  173.7 3.4 %copy-start.2 = (f32[4,128,12,128]{1,3,2,0:T(8,128)S(1)}, f32[4,128,12,128]{1,3,2,0:T(8,128)}, u32[]{:S(2)}) copy-start(f32[4,128,12,128]{1,3,2,0:T(8,128)} %get-tuple-element.195) | copy-start | bytes 9437188 | tf_op jit(solution)/shard_map/while
  187.9 2.0 copy-start.1
  193.8 3.4 %copy-start.2 = (f32[4,128,12,128]{1,3,2,0:T(8,128)S(1)}, f32[4,128,12,128]{1,3,2,0:T(8,128)}, u32[]{:S(2)}) copy-start(f32[4,128,12,128]{1,3,2,0:T(8,128)} %get-tuple-element.195) | copy-start | bytes 9437188 | tf_op jit(solution)/shard_map/while
  207.9 2.0 copy-start.1
  213.8 3.4 %copy-start.2 = (f32[4,128,12,128]{1,3,2,0:T(8,128)S(1)}, f32[4,128,12,128]{1,3,2,0:T(8,128)}, u32[]{:S(2)}) copy-start(f32[4,128,12,128]{1,3,2,0:T(8,128)} %get-tuple-element.195) | copy-start | bytes 9437188 | tf_op jit(solution)/shard_map/while
  227.9 2.0 copy-start.1
  233.8 3.4 %copy-start.2 = (f32[4,128,12,128]{1,3,2,0:T(8,128)S(1)}, f32[4,128,12,128]{1,3,2,0:T(8,128)}, u32[]{:S(2)}) copy-start(f32[4,128,12,128]{1,3,2,0:T(8,128)} %get-tuple-element.195) | copy-start | bytes 9437188 | tf_op jit(solution)/shard_map/while
  247.9 2.0 copy-start.1
  253.8 3.4 %copy-start.2 = (f32[4,128,12,128]{1,3,2,0:T(8,128)S(1)}, f32[4,128,12,128]{1,3,2,0:T(8,128)}, u32[]{:S(2)}) copy-start(f32[4,128,12,128]{1,3,2,0:T(8,128)} %get-tuple-element.195) | copy-start | bytes 9437188 | tf_op jit(solution)/shard_map/while
Sparse Core Ops, SparseCore 0:
  26.3 28.9 all-gather.1
where the time goes:
time: 311 us; the launch traced here: 309 us
  local copies, waits for them, and re-layouts  101 us (32%)
  matrix products  67.9 us (22%)
  waiting for transfers between devices  65.1 us (21%)
  blocking collectives  34.9 us (11%)
  other arithmetic  13.9 us (4%)
  between operations  13.5 us (4%)
  starting transfers between devices  11.8 us (4%)
    all_to_all x1, waiting for transfers between devices, per_device(): lax.all_to_all(shaped, 'seq', split_axis=2, concat_axis=0, tiled=True)  36.5 us
    all_to_all x1, blocking collectives, per_device(): lax.all_to_all(attended, 'seq', split_axis=0, concat_axis=1, tiled=True)  34.9 us
    all_gather x1, waiting for transfers between devices, per_device(): kept_all = lax.all_gather(kept_kv, 'blk', axis=0, tiled=True)  28.6 us
    gather x8, local copies, waits for them, and re-layouts, attend(): far_values = far_values_all[kept_sel]  27.3 us
    dot_general x8, matrix products, attend(): jnp.einsum('bhiwk,bwhkd->bhid', far_weights.astype(jnp.bfloat16), far_val...  25.9 us
    dot_general x8, matrix products, attend(): jnp.einsum('bhid,bwhkd->bhiwk', queries, far_keys, preferred_element_type...  25.1 us
    gather x8, local copies, waits for them, and re-layouts, attend(): far_keys = far_keys_all[kept_sel]  16.6 us
    gather x8, local copies, waits for them, and re-layouts, attend(): near_values = near_values_all[cur_sel]  15.8 us
  transfers between devices with their start and end apart: 2, of which 2 were waited for; matrix products, arithmetic and copies ran while one was open for 2% of the time, Pallas kernels for 0%

commit v1 on v0

--- a/solution.py
+++ b/solution.py
@@ -25,7 +25,15 @@
     queries_all = ordered[0]
     near_keys_all = ordered[1]
     near_values_all = ordered[2]
-    kept_all = lax.all_gather(kept_kv, "blk", axis=0, tiled=True)
+    kept_all = jnp.concatenate(
+        lax.all_to_all(
+            jnp.stack([kept_kv for _ in range(lax.axis_size("blk"))]),
+            axis_name="blk",
+            split_axis=0,
+            concat_axis=0,
+        ),
+        0,
+    )
     kept_all = jnp.transpose(
         kept_all.reshape(kept_all.shape[0], 2, tile_len, head_dev, head_width), (0, 1, 3, 2, 4)
     )

time: 311 us -> 325 us (1.045)
  waiting for transfers between devices: 65.1 us -> 87.2 us
  between operations: 13.5 us -> 0.13 us
  starting transfers between devices: 11.8 us -> 16.1 us
    all_to_all x1, waiting for transfers between devices: 36.5 us -> 65.3 us  [per_device(): lax.all_to_all(shaped, 'seq', split_axis=2, concat_axis=0, tiled=True)]
    all_gather x1 -> x0, waiting for transfers between devices: 28.6 us -> none  [per_device(): kept_all = lax.all_gather(kept_kv, 'blk', axis=0, tiled=True)]
    all_to_all x0 -> x1, waiting for transfers between devices: none -> 21.9 us  [per_device(): lax.all_to_all(jnp.stack([kept_kv for _ in range(lax.axis_size('blk'))]),...]
    all_to_all x0 -> x1, starting transfers between devices: none -> 4.47 us  [per_device(): lax.all_to_all(jnp.stack([kept_kv for _ in range(lax.axis_size('blk'))]),...]
  transfers between devices with their start and end apart: 2 -> 2, of which waited for: 2 -> 2; matrix products, arithmetic and copies ran while one was open for 2% -> 3% of each run, Pallas kernels for 0% -> 0%
where the time goes in v1:
time: 325 us; the launch traced here: 323 us
  local copies, waits for them, and re-layouts  103 us (32%)
  waiting for transfers between devices  87.2 us (27%)
  matrix products  68 us (21%)
  blocking collectives  34.5 us (11%)
  starting transfers between devices  16.1 us (5%)
  other arithmetic  13.9 us (4%)
    all_to_all x1, waiting for transfers between devices, per_device(): lax.all_to_all(shaped, 'seq', split_axis=2, concat_axis=0, tiled=True)  65.3 us
    all_to_all x1, blocking collectives, per_device(): lax.all_to_all(attended, 'seq', split_axis=0, concat_axis=1, tiled=True)  34.5 us
    gather x8, local copies, waits for them, and re-layouts, attend(): far_values = far_values_all[kept_sel]  26.6 us
    dot_general x8, matrix products, attend(): jnp.einsum('bhiwk,bwhkd->bhid', far_weights.astype(jnp.bfloat16), far_val...  25.9 us
    dot_general x8, matrix products, attend(): jnp.einsum('bhid,bwhkd->bhiwk', queries, far_keys, preferred_element_type...  25.2 us
    all_to_all x1, waiting for transfers between devices, per_device(): lax.all_to_all(jnp.stack([kept_kv for _ in range(lax.axis_size('blk'))]),...  21.9 us
    gather x8, local copies, waits for them, and re-layouts, attend(): far_keys = far_keys_all[kept_sel]  16.6 us
    gather x8, local copies, waits for them, and re-layouts, attend(): near_values = near_values_all[cur_sel]  15.8 us
  transfers between devices with their start and end apart: 2, of which 2 were waited for; matrix products, arithmetic and copies ran while one was open for 3% of the time, Pallas kernels for 0%

profile of v1, /device:TPU:2, one launch (start us, length us, event | category | flops | bytes accessed | tf_op | source)
XLA Modules:
  0.0 323.1 jit_solution(12953275607247200835)
XLA Ops:
  2.9 4.5 %all-to-all-start.1 = ((bf16[8,4,2,128,128]{4,3,1,2,0:T(8,128)(2,1)}), bf16[8,4,2,128,128]{4,3,1,2,0:T(8,128)(2,1)}, u32[]{:S(2)}, u32[]{:S(2)}) async-start(bf16[8,4,2,128,128]{4,3,1,2,0:T(8,128)(2,1)} %stack.2), calls=%async_computation.1 | async-start | bytes 4194304 | tf_op jit(solution)/shard_map/all_to_all | solution.py:29
  7.3 3.5 %copy.45 = bf16[128,12288]{0,1:T(8,128)(2,1)S(1)} copy(bf16[128,12288]{1,0:T(8,128)(2,1)} %param.7) | data formatting | bytes 6291456 | tf_op args[0]
  12.7 21.9 %all-to-all-done.1 = bf16[8,4,2,128,128]{4,3,1,2,0:T(8,128)(2,1)} async-done(((bf16[8,4,2,128,128]{4,3,1,2,0:T(8,128)(2,1)}), bf16[8,4,2,128,128]{4,3,1,2,0:T(8,128)(2,1)}, u32[]{:S(2)}, u32[]{:S(2)}) %all-to-all-start.1) | async-done | bytes 2097184 | tf_op jit(solution)/shard_map/all_to_all | solution.py:29
  34.6 11.6 %all-to-all-start = ((bf16[128,3,32,128]{0,3,1,2:T(8,128)(2,1)}), bf16[128,3,32,128]{0,3,1,2:T(8,128)(2,1)S(1)}, u32[]{:S(2)}, u32[]{:S(2)}) async-start(bf16[128,3,32,128]{0,3,1,2:T(8,128)(2,1)} %copy.46), calls=%async_computation | async-start | bytes 6291456 | tf_op jit(solution)/shard_map/all_to_all | solution.py:20
  51.7 65.3 %all-to-all-done = bf16[128,3,32,128]{0,3,1,2:T(8,128)(2,1)S(1)} async-done(((bf16[128,3,32,128]{0,3,1,2:T(8,128)(2,1)}), bf16[128,3,32,128]{0,3,1,2:T(8,128)(2,1)S(1)}, u32[]{:S(2)}, u32[]{:S(2)}) %all-to-all-start) | async-done | bytes 3145760 | tf_op jit(solution)/shard_map/all_to_all | solution.py:20
  122.5 159.6 %while.10 = (s32[]{:T(128)}, bf16[8,4,128,1,128]{4,2,1,3,0:T(8,128)(2,1)}, bf16[8,4,1,128,128]{3,4,1,0,2:T(8,128)(2,1)}, s32[8,4,8]{2,1,0:T(4,128)S(1)}, bf16[32...) while((s32[]{:T(128)}, ...), condition=%wide.region_5.6_spmd, body=%wide.region_0.5_spmd.sunk | while | flops 685704448 | bytes 57583712 | solution.py:91
  135.9 3.3 %gather_fusion.3 = bf16[48,128,128]{2,1,0:T(8,128)(2,1)} fusion(bf16[32,128,128]{2,1,0:T(8,128)(2,1)} %bitcast.127, s32[1024]{0:T(1024)S(1)} %pad_clamp_fusion.6), kind=kCustom, calls=%fused_computation.3.clone.1 | custom fusion | bytes 3145920 | tf_op jit(solution)/shard_map/while/body/eval_jaxpr/gather | solution.py:65
  139.2 3.2 %fusion.70 = bf16[8,4,128,1,128]{4,2,1,3,0:T(8,128)(2,1)} fusion(bf16[8,4,128,1,128]{4,2,1,3,0:T(8,128)(2,1)} %get-tuple-element.208, s32[]{:T(128)} %get-tuple-element.207, f32[4,128,128]{2,1,0:T(8,128)S(1)} %convolution_bitcast_fusion.2, bf16[4,12,128,128]{3,2,1,0:T(8,128)(2,1)} %bitcast.128, f32[4,128,12,128]{1,3,2,0:T(8,128)S(1)} %copy-done.2, ...), kind=kOutput, calls=%fused_computation.24.clone.1 | convolution fusion | flops 205455360 | bytes 5116464 | tf_op jit(solution)/shard_map/while/body/eval_jaxpr/bhiwk,bwhkd->bhid/dot_general | solution.py:82
  144.7 3.1 fusion.67
  155.8 3.3 %gather_fusion.3 = bf16[48,128,128]{2,1,0:T(8,128)(2,1)} fusion(bf16[32,128,128]{2,1,0:T(8,128)(2,1)} %bitcast.127, s32[1024]{0:T(1024)S(1)} %pad_clamp_fusion.6), kind=kCustom, calls=%fused_computation.3.clone.1 | custom fusion | bytes 3145920 | tf_op jit(solution)/shard_map/while/body/eval_jaxpr/gather | solution.py:65
  159.1 3.2 %fusion.70 = bf16[8,4,128,1,128]{4,2,1,3,0:T(8,128)(2,1)} fusion(bf16[8,4,128,1,128]{4,2,1,3,0:T(8,128)(2,1)} %get-tuple-element.208, s32[]{:T(128)} %get-tuple-element.207, f32[4,128,128]{2,1,0:T(8,128)S(1)} %convolution_bitcast_fusion.2, bf16[4,12,128,128]{3,2,1,0:T(8,128)(2,1)} %bitcast.128, f32[4,128,12,128]{1,3,2,0:T(8,128)S(1)} %copy-done.2, ...), kind=kOutput, calls=%fused_computation.24.clone.1 | convolution fusion | flops 205455360 | bytes 5116464 | tf_op jit(solution)/shard_map/while/body/eval_jaxpr/bhiwk,bwhkd->bhid/dot_general | solution.py:82
  175.8 3.3 %gather_fusion.3 = bf16[48,128,128]{2,1,0:T(8,128)(2,1)} fusion(bf16[32,128,128]{2,1,0:T(8,128)(2,1)} %bitcast.127, s32[1024]{0:T(1024)S(1)} %pad_clamp_fusion.6), kind=kCustom, calls=%fused_computation.3.clone.1 | custom fusion | bytes 3145920 | tf_op jit(solution)/shard_map/while/body/eval_jaxpr/gather | solution.py:65
  179.1 3.2 %fusion.70 = bf16[8,4,128,1,128]{4,2,1,3,0:T(8,128)(2,1)} fusion(bf16[8,4,128,1,128]{4,2,1,3,0:T(8,128)(2,1)} %get-tuple-element.208, s32[]{:T(128)} %get-tuple-element.207, f32[4,128,128]{2,1,0:T(8,128)S(1)} %convolution_bitcast_fusion.2, bf16[4,12,128,128]{3,2,1,0:T(8,128)(2,1)} %bitcast.128, f32[4,128,12,128]{1,3,2,0:T(8,128)S(1)} %copy-done.2, ...), kind=kOutput, calls=%fused_computation.24.clone.1 | convolution fusion | flops 205455360 | bytes 5116464 | tf_op jit(solution)/shard_map/while/body/eval_jaxpr/bhiwk,bwhkd->bhid/dot_general | solution.py:82
  195.7 3.3 %gather_fusion.3 = bf16[48,128,128]{2,1,0:T(8,128)(2,1)} fusion(bf16[32,128,128]{2,1,0:T(8,128)(2,1)} %bitcast.127, s32[1024]{0:T(1024)S(1)} %pad_clamp_fusion.6), kind=kCustom, calls=%fused_computation.3.clone.1 | custom fusion | bytes 3145920 | tf_op jit(solution)/shard_map/while/body/eval_jaxpr/gather | solution.py:65
  199.0 3.2 %fusion.70 = bf16[8,4,128,1,128]{4,2,1,3,0:T(8,128)(2,1)} fusion(bf16[8,4,128,1,128]{4,2,1,3,0:T(8,128)(2,1)} %get-tuple-element.208, s32[]{:T(128)} %get-tuple-element.207, f32[4,128,128]{2,1,0:T(8,128)S(1)} %convolution_bitcast_fusion.2, bf16[4,12,128,128]{3,2,1,0:T(8,128)(2,1)} %bitcast.128, f32[4,128,12,128]{1,3,2,0:T(8,128)S(1)} %copy-done.2, ...), kind=kOutput, calls=%fused_computation.24.clone.1 | convolution fusion | flops 205455360 | bytes 5116464 | tf_op jit(solution)/shard_map/while/body/eval_jaxpr/bhiwk,bwhkd->bhid/dot_general | solution.py:82
  215.7 3.3 %gather_fusion.3 = bf16[48,128,128]{2,1,0:T(8,128)(2,1)} fusion(bf16[32,128,128]{2,1,0:T(8,128)(2,1)} %bitcast.127, s32[1024]{0:T(1024)S(1)} %pad_clamp_fusion.6), kind=kCustom, calls=%fused_computation.3.clone.1 | custom fusion | bytes 3145920 | tf_op jit(solution)/shard_map/while/body/eval_jaxpr/gather | solution.py:65
  219.0 3.2 %fusion.70 = bf16[8,4,128,1,128]{4,2,1,3,0:T(8,128)(2,1)} fusion(bf16[8,4,128,1,128]{4,2,1,3,0:T(8,128)(2,1)} %get-tuple-element.208, s32[]{:T(128)} %get-tuple-element.207, f32[4,128,128]{2,1,0:T(8,128)S(1)} %convolution_bitcast_fusion.2, bf16[4,12,128,128]{3,2,1,0:T(8,128)(2,1)} %bitcast.128, f32[4,128,12,128]{1,3,2,0:T(8,128)S(1)} %copy-done.2, ...), kind=kOutput, calls=%fused_computation.24.clone.1 | convolution fusion | flops 205455360 | bytes 5116464 | tf_op jit(solution)/shard_map/while/body/eval_jaxpr/bhiwk,bwhkd->bhid/dot_general | solution.py:82
  235.6 3.3 %gather_fusion.3 = bf16[48,128,128]{2,1,0:T(8,128)(2,1)} fusion(bf16[32,128,128]{2,1,0:T(8,128)(2,1)} %bitcast.127, s32[1024]{0:T(1024)S(1)} %pad_clamp_fusion.6), kind=kCustom, calls=%fused_computation.3.clone.1 | custom fusion | bytes 3145920 | tf_op jit(solution)/shard_map/while/body/eval_jaxpr/gather | solution.py:65
  238.9 3.2 %fusion.70 = bf16[8,4,128,1,128]{4,2,1,3,0:T(8,128)(2,1)} fusion(bf16[8,4,128,1,128]{4,2,1,3,0:T(8,128)(2,1)} %get-tuple-element.208, s32[]{:T(128)} %get-tuple-element.207, f32[4,128,128]{2,1,0:T(8,128)S(1)} %convolution_bitcast_fusion.2, bf16[4,12,128,128]{3,2,1,0:T(8,128)(2,1)} %bitcast.128, f32[4,128,12,128]{1,3,2,0:T(8,128)S(1)} %copy-done.2, ...), kind=kOutput, calls=%fused_computation.24.clone.1 | convolution fusion | flops 205455360 | bytes 5116464 | tf_op jit(solution)/shard_map/while/body/eval_jaxpr/bhiwk,bwhkd->bhid/dot_general | solution.py:82
  255.6 3.3 %gather_fusion.3 = bf16[48,128,128]{2,1,0:T(8,128)(2,1)} fusion(bf16[32,128,128]{2,1,0:T(8,128)(2,1)} %bitcast.127, s32[1024]{0:T(1024)S(1)} %pad_clamp_fusion.6), kind=kCustom, calls=%fused_computation.3.clone.1 | custom fusion | bytes 3145920 | tf_op jit(solution)/shard_map/while/body/eval_jaxpr/gather | solution.py:65
  258.9 3.2 %fusion.70 = bf16[8,4,128,1,128]{4,2,1,3,0:T(8,128)(2,1)} fusion(bf16[8,4,128,1,128]{4,2,1,3,0:T(8,128)(2,1)} %get-tuple-element.208, s32[]{:T(128)} %get-tuple-element.207, f32[4,128,128]{2,1,0:T(8,128)S(1)} %convolution_bitcast_fusion.2, bf16[4,12,128,128]{3,2,1,0:T(8,128)(2,1)} %bitcast.128, f32[4,128,12,128]{1,3,2,0:T(8,128)S(1)} %copy-done.2, ...), kind=kOutput, calls=%fused_computation.24.clone.1 | convolution fusion | flops 205455360 | bytes 5116464 | tf_op jit(solution)/shard_map/while/body/eval_jaxpr/bhiwk,bwhkd->bhid/dot_general | solution.py:82
  275.5 3.3 %gather_fusion.3 = bf16[48,128,128]{2,1,0:T(8,128)(2,1)} fusion(bf16[32,128,128]{2,1,0:T(8,128)(2,1)} %bitcast.127, s32[1024]{0:T(1024)S(1)} %pad_clamp_fusion.6), kind=kCustom, calls=%fused_computation.3.clone.1 | custom fusion | bytes 3145920 | tf_op jit(solution)/shard_map/while/body/eval_jaxpr/gather | solution.py:65
  278.8 3.2 %fusion.70 = bf16[8,4,128,1,128]{4,2,1,3,0:T(8,128)(2,1)} fusion(bf16[8,4,128,1,128]{4,2,1,3,0:T(8,128)(2,1)} %get-tuple-element.208, s32[]{:T(128)} %get-tuple-element.207, f32[4,128,128]{2,1,0:T(8,128)S(1)} %convolution_bitcast_fusion.2, bf16[4,12,128,128]{3,2,1,0:T(8,128)(2,1)} %bitcast.128, f32[4,128,12,128]{1,3,2,0:T(8,128)S(1)} %copy-done.2, ...), kind=kOutput, calls=%fused_computation.24.clone.1 | convolution fusion | flops 205455360 | bytes 5116464 | tf_op jit(solution)/shard_map/while/body/eval_jaxpr/bhiwk,bwhkd->bhid/dot_general | solution.py:82
  285.4 34.5 %all_to_all.32 = bf16[32,2,8192]{2,1,0:T(2,128)(2,1)S(1)} all-to-all(bf16[32,2,8192]{2,1,0:T(2,128)(2,1)S(1)} %reshape.278), channel_id=1, replica_groups=mesh['seq'=32,'blk'=8] {'seq'}, dimensions={0} | all-to-all | bytes 2097152 | tf_op jit(solution)/shard_map/all_to_all | solution.py:101
  (208 shorter events, 125.4 us)
Async XLA Ops:
  0.0 47.7 %copy-start = (s32[256]{0:T(256)S(1)}, s32[256]{0:T(256)}, u32[]{:S(2)}) copy-start(s32[256]{0:T(256)} %param.11) | copy-start | bytes 3076
  2.9 31.7 %all-to-all-start.1 = ((bf16[8,4,2,128,128]{4,3,1,2,0:T(8,128)(2,1)}), bf16[8,4,2,128,128]{4,3,1,2,0:T(8,128)(2,1)}, u32[]{:S(2)}, u32[]{:S(2)}) async-start(bf16[8,4,2,128,128]{4,3,1,2,0:T(8,128)(2,1)} %stack.2), calls=%async_computation.1 | async-start | bytes 4194304 | tf_op jit(solution)/shard_map/all_to_all | solution.py:29
  12.7 33.5 %copy-start.5 = (s32[256,8]{0,1:T(8,128)S(1)}, s32[256,8]{0,1:T(8,128)}, u32[]{:S(2)}) copy-start(s32[256,8]{0,1:T(8,128)} %param.9) | copy-start | bytes 24580
  12.7 33.7 %copy-start.4 = (s32[256,12]{0,1:T(8,128)S(1)}, s32[256,12]{0,1:T(8,128)}, u32[]{:S(2)}) copy-start(s32[256,12]{0,1:T(8,128)} %param.10) | copy-start | bytes 36868
  34.6 82.4 %all-to-all-start = ((bf16[128,3,32,128]{0,3,1,2:T(8,128)(2,1)}), bf16[128,3,32,128]{0,3,1,2:T(8,128)(2,1)S(1)}, u32[]{:S(2)}, u32[]{:S(2)}) async-start(bf16[128,3,32,128]{0,3,1,2:T(8,128)(2,1)} %copy.46), calls=%async_computation | async-start | bytes 6291456 | tf_op jit(solution)/shard_map/all_to_all | solution.py:20
  118.7 2.4 copy-start.3
  130.0 2.0 copy-start.1
  135.8 3.3 %copy-start.2 = (f32[4,128,12,128]{1,3,2,0:T(8,128)S(1)}, f32[4,128,12,128]{1,3,2,0:T(8,128)}, u32[]{:S(2)}) copy-start(f32[4,128,12,128]{1,3,2,0:T(8,128)} %get-tuple-element.195) | copy-start | bytes 9437188 | tf_op jit(solution)/shard_map/while
  149.9 2.0 copy-start.1
  155.8 3.3 %copy-start.2 = (f32[4,128,12,128]{1,3,2,0:T(8,128)S(1)}, f32[4,128,12,128]{1,3,2,0:T(8,128)}, u32[]{:S(2)}) copy-start(f32[4,128,12,128]{1,3,2,0:T(8,128)} %get-tuple-element.195) | copy-start | bytes 9437188 | tf_op jit(solution)/shard_map/while
  169.9 2.0 copy-start.1
  175.7 3.3 %copy-start.2 = (f32[4,128,12,128]{1,3,2,0:T(8,128)S(1)}, f32[4,128,12,128]{1,3,2,0:T(8,128)}, u32[]{:S(2)}) copy-start(f32[4,128,12,128]{1,3,2,0:T(8,128)} %get-tuple-element.195) | copy-start | bytes 9437188 | tf_op jit(solution)/shard_map/while
  189.8 2.0 copy-start.1
  195.7 3.3 %copy-start.2 = (f32[4,128,12,128]{1,3,2,0:T(8,128)S(1)}, f32[4,128,12,128]{1,3,2,0:T(8,128)}, u32[]{:S(2)}) copy-start(f32[4,128,12,128]{1,3,2,0:T(8,128)} %get-tuple-element.195) | copy-start | bytes 9437188 | tf_op jit(solution)/shard_map/while
  209.8 2.0 copy-start.1
  215.6 3.3 %copy-start.2 = (f32[4,128,12,128]{1,3,2,0:T(8,128)S(1)}, f32[4,128,12,128]{1,3,2,0:T(8,128)}, u32[]{:S(2)}) copy-start(f32[4,128,12,128]{1,3,2,0:T(8,128)} %get-tuple-element.195) | copy-start | bytes 9437188 | tf_op jit(solution)/shard_map/while
  229.7 2.0 copy-start.1
  235.6 3.3 %copy-start.2 = (f32[4,128,12,128]{1,3,2,0:T(8,128)S(1)}, f32[4,128,12,128]{1,3,2,0:T(8,128)}, u32[]{:S(2)}) copy-start(f32[4,128,12,128]{1,3,2,0:T(8,128)} %get-tuple-element.195) | copy-start | bytes 9437188 | tf_op jit(solution)/shard_map/while
  249.7 2.0 copy-start.1
  255.5 3.3 %copy-start.2 = (f32[4,128,12,128]{1,3,2,0:T(8,128)S(1)}, f32[4,128,12,128]{1,3,2,0:T(8,128)}, u32[]{:S(2)}) copy-start(f32[4,128,12,128]{1,3,2,0:T(8,128)} %get-tuple-element.195) | copy-start | bytes 9437188 | tf_op jit(solution)/shard_map/while
  269.6 2.0 copy-start.1
  275.5 3.3 %copy-start.2 = (f32[4,128,12,128]{1,3,2,0:T(8,128)S(1)}, f32[4,128,12,128]{1,3,2,0:T(8,128)}, u32[]{:S(2)}) copy-start(f32[4,128,12,128]{1,3,2,0:T(8,128)} %get-tuple-element.195) | copy-start | bytes 9437188 | tf_op jit(solution)/shard_map/while
